TPU v7x, 32 devices: a whole 2x2x4 slice. The times are simulated.
32 devices in a mesh: cell: 2 (over x), occ: 16 (over z, y, core).
Axes of the slice: x: 2, y: 2, z: 4, core: 2. Of those that a mesh axis runs over, the one named last changes fastest.
Arguments:
- factors: bfloat16 [12288, 16, 512], P('cell', 'occ'), parts along dimension 0, may hold values from -1.02 to 1.02
- gap_index: int32 [32, 512], P('cell'), parts along dimension 0, may hold values from 0 to 63
- gap_table: float32 [128], P('cell'), parts along dimension 0, may hold values from 0.25 to 2
- pair_level: int32 [32, 1], P('cell'), parts along dimension 0, may hold values from 0 to 7
- pair_shift: float32 [8], replicated, may hold values from 0.5 to 4
Outputs:
- gradient_factors: bfloat16 [12288, 16, 512], P('cell', 'occ'), parts along dimension 0
- pair_energy: float32 [2], P('cell'), parts along dimension 0
There are 2 independent parts, one for each index of `cell`. A program takes and returns all parts, laid end to end along the dimension named above; an argument that names none is the same for every part. Nothing has to cross between parts.
All inputs are finite; a program needn't handle non-finite values.
Results may differ from a plain program's by a relative error of at most 0.0053.
Values may be sent and summed in bfloat16 or wider, within the bound.
A program may use at most 128 MiB of HBM per device.

v0:
```python
import jax
import jax.numpy as jnp
from jax import lax
from jax.sharding import PartitionSpec as P

STEPS = 1


def from_behind(value, axis, steps):
    count = lax.axis_size(axis)
    pairs = [(source, (source + steps) % count) for source in range(count)]
    return lax.ppermute(value, axis, pairs)


def block_gaps(gap_index, gap_table, block_number, occ_count):
    picked = lax.dynamic_slice_in_dim(gap_index, block_number * occ_count, occ_count, 0).reshape(-1)
    levels = jnp.arange(gap_table.shape[0], dtype=jnp.int32)
    return jnp.sum(jnp.where(levels[:, None] == picked[None, :], gap_table[:, None], 0.0), axis=0)


def level_value(pair_level, pair_shift, block_number):
    chosen = lax.dynamic_slice(pair_level, (block_number, 0), (1, 1))[0, 0]
    levels = jnp.arange(pair_shift.shape[0], dtype=jnp.int32)
    return jnp.sum(jnp.where(levels == chosen, pair_shift, 0.0))


def amplitudes(left_block, right_block, left_gap, right_gap, shift_value):
    pairs = lax.dot_general(
        left_block, right_block, (((0,), (0,)), ((), ())), preferred_element_type=jnp.float32
    )
    amplitude = pairs / (left_gap[:, None] + right_gap[None, :] + shift_value)
    return (amplitude, jnp.sum(amplitude * pairs))


def on_device(factors, gap_index, gap_table, pair_level, pair_shift):
    aux_rows, occ_count, virtuals = factors.shape
    columns = occ_count * virtuals
    blocks = lax.axis_size("occ")
    position = lax.axis_index("occ")
    own_block = factors.reshape(aux_rows, columns)
    own_gap = block_gaps(gap_index, gap_table, position, occ_count)
    visiting = own_block
    visiting = from_behind(visiting, "occ", 1)
    partner = jnp.mod(position - 1, blocks)
    partner_gap = block_gaps(gap_index, gap_table, partner, occ_count)
    shift_value = level_value(pair_level, pair_shift, position)
    amplitude, pair_sum = amplitudes(own_block, visiting, own_gap, partner_gap, shift_value)
    amp_low = amplitude.astype(jnp.bfloat16)
    gradient = lax.dot_general(
        visiting, amp_low, (((1,), (1,)), ((), ())), preferred_element_type=jnp.float32
    )
    outgoing = jnp.dot(own_block, amp_low, preferred_element_type=jnp.float32).astype(jnp.bfloat16)
    incoming = from_behind(outgoing, "occ", -1)
    gradient = gradient + incoming.astype(jnp.float32)
    total = lax.psum(pair_sum, "occ")
    pair_energy = (total * (-1.3 / (blocks * STEPS * columns * columns))).reshape(1)
    return (gradient.astype(jnp.bfloat16).reshape(aux_rows, occ_count, virtuals), pair_energy)


def solution(mesh):
    in_specs = (P("cell", "occ", None), P("cell", None), P("cell"), P("cell", None), P())
    out_specs = (P("cell", "occ", None), P("cell"))
    return jax.shard_map(
        on_device, mesh=mesh, in_specs=in_specs, out_specs=out_specs, check_vma=False
    )
```

profile of v0, /device:TPU:0, one launch (start us, length us, event | category | flops | bytes accessed | tf_op | source)
XLA Modules:
  0.0 208.3 jit_solution(13996598571460671999)
XLA Ops:
  0.6 0.0 copy-start
  0.6 0.5 collective-permute-start
  1.2 0.1 copy-done
  1.3 0.6 constant_dynamic-slice_fusion
  1.9 0.7 constant_dynamic-slice_fusion.1
  2.6 1.9 fusion.4
  4.6 0.8 select_reduce_fusion.1
  5.3 69.8 %collective-permute-done = bf16[6144,512]{1,0:T(8,128)(2,1)} collective-permute-done((bf16[6144,512]{1,0:T(8,128)(2,1)}, bf16[6144,512]{1,0:T(8,128)(2,1)}, u32[]{:S(2)}, u32[]{:S(2)}) %collective-permute-start) | collective-permute-done | bytes 6291488 | tf_op jit(solution)/shard_map/ppermute | solution.py:12
  75.2 0.0 copy-start.1
  75.2 9.9 %multiply_reduce_fusion = (f32[]{:T(128)}, f32[512,512]{1,0:T(8,128)S(1)}) fusion(f32[]{:T(128)} %fusion.4, f32[512]{0:T(512)S(1)} %get-tuple-element.7, f32[512]{0:T(512)S(1)} %get-tuple-element.6, bf16[6144,512]{1,0:T(8,128)(2,1)} %collective-permute-done, bf16[6144,1,512]{2,0,1:T(8,128)(2,1)} %param.5), kind=kOutput, calls=%fused_computation.5 | convolution fusion | flops 3222536192 | bytes 13635592 | tf_op jit(solution)/shard_map/dot_general | solution.py:28
  85.1 0.0 copy-done.1
  85.1 6.5 %fusion.1 = bf16[6144,512]{0,1:T(8,128)(2,1)} fusion(bf16[6144,1,512]{2,0,1:T(8,128)(2,1)S(1)} %copy-done.1, f32[512,512]{1,0:T(8,128)S(1)} %get-tuple-element.11, f32[]{:T(128)} %fusion.4, f32[512]{0:T(512)S(1)} %get-tuple-element.7, f32[512]{0:T(512)S(1)} %get-tuple-element.6), kind=kOutput, calls=%fused_computation.3 | convolution fusion | flops 3225419776 | bytes 13635588 | tf_op jit(solution)/shard_map/dot_general | solution.py:52
  91.6 0.0 collective-permute-start.1
  91.6 96.4 %psum.7 = f32[]{:T(128)} all-reduce(f32[]{:T(128)} %get-tuple-element.10), channel_id=1, replica_groups=mesh['cell'=2,'occ'=16] {'occ'}, use_global_device_ids=true, to_apply=%region_4.5 | all-reduce | flops 1 | bytes 8 | tf_op jit(solution)/shard_map/psum | solution.py:55
  188.6 0.0 collective-permute-done.1
  188.7 9.8 %fusion.2 = bf16[6144,1,512]{0,2,1:T(8,128)(2,1)} fusion(bf16[6144,512]{0,1:T(8,128)(2,1)} %collective-permute-done.1, bf16[6144,512]{1,0:T(8,128)(2,1)} %collective-permute-done, f32[512,512]{1,0:T(8,128)S(1)} %get-tuple-element.11, f32[]{:T(128)} %fusion.4, f32[512]{0:T(512)S(1)} %get-tuple-element.7, f32[512]{0:T(512)S(1)} %get-tuple-element.6), kind=kOutput, calls=%fused_computation.4 | convolution fusion | flops 3231711232 | bytes 19927044 | tf_op jit(solution)/shard_map/dot_general | solution.py:49
  198.5 8.6 %copy.8 = bf16[6144,1,512]{2,0,1:T(8,128)(2,1)} copy(bf16[6144,1,512]{0,2,1:T(8,128)(2,1)} %fusion.2) | data formatting | bytes 12582912
Async XLA Ops:
  0.6 0.7 copy-start
  0.6 74.5 %collective-permute-start = (bf16[6144,512]{1,0:T(8,128)(2,1)}, bf16[6144,512]{1,0:T(8,128)(2,1)}, u32[]{:S(2)}, u32[]{:S(2)}) collective-permute-start(bf16[6144,512]{1,0:T(8,128)(2,1)} %bitcast.25), channel_id=1, source_target_pairs={{0,1},{1,2},{2,3},{3,4},{4,5},{5,6},{6,7},{7,8},{8,9},{9,10},{10,1... | collective-permute-start | bytes 18874376 | tf_op jit(solution)/shard_map/ppermute | solution.py:12
  75.2 9.9 %copy-start.1 = (bf16[6144,1,512]{2,0,1:T(8,128)(2,1)S(1)}, bf16[6144,1,512]{2,0,1:T(8,128)(2,1)}, u32[]{:S(2)}) copy-start(bf16[6144,1,512]{2,0,1:T(8,128)(2,1)} %param.5) | copy-start | bytes 18874372
  91.6 97.1 %collective-permute-start.1 = (bf16[6144,512]{0,1:T(8,128)(2,1)}, bf16[6144,512]{0,1:T(8,128)(2,1)}, u32[]{:S(2)}, u32[]{:S(2)}) collective-permute-start(bf16[6144,512]{0,1:T(8,128)(2,1)} %fusion.1), channel_id=1, source_target_pairs={{0,15},{1,0},{2,1},{3,2},{4,3},{5,4},{6,5},{7,6},{8,7},{9,8},{10,9... | collective-permute-start | bytes 18874376 | tf_op jit(solution)/shard_map/ppermute | solution.py:12
where the time goes:
time: 209 us; the launch traced here: 208 us
  blocking collectives  96.4 us (46%)
  waiting for transfers between devices  69.8 us (33%)
  matrix products  26.3 us (13%)
  local copies, waits for them, and re-layouts  10.1 us (5%)
  other arithmetic  2.7 us (1%)
  between operations  2.44 us (1%)
    psum x1, blocking collectives, on_device(): total = lax.psum(pair_sum, 'occ')  96.4 us
    ppermute x2, waiting for transfers between devices, from_behind(): return lax.ppermute(value, axis, pairs)  69.8 us
    dot_general x1, matrix products, amplitudes(): lax.dot_general(left_block, right_block, (((0,), (0,)), ((), ())), prefer...  9.94 us
    dot_general x1, matrix products, on_device(): lax.dot_general(visiting, amp_low, (((1,), (1,)), ((), ())), preferred_el...  9.84 us
    unnamed x5, local copies, waits for them, and re-layouts  8.74 us
    dot_general x1, matrix products, on_device(): jnp.dot(own_block, amp_low, preferred_element_type=jnp.float32)  6.48 us
  transfers between devices with their start and end apart: 2, of which 1 were waited for; matrix products, arithmetic and copies ran while one was open for 2% of the time, Pallas kernels for 0%

commit v1 on v0

v1 whole, which is shorter than its diff:
```python
import functools

import jax
import jax.numpy as jnp
from jax import lax
from jax.experimental import pallas as pl
from jax.experimental.pallas import tpu as pltpu
from jax.sharding import PartitionSpec as P

STEPS = 1
MESH = pl.DeviceIdType.MESH
CHUNK_ROWS = 128


def chunk_rows_of(aux_rows):
    rows = min(CHUNK_ROWS, aux_rows)
    while aux_rows % rows:
        rows -= 16
    return rows


def kernel(
    blocks, rows, scale,
    f_ref, index_ref, table_ref, level_ref, shift_ref,
    out_ref, energy_ref,
    own, visiting, outgoing, incoming, nearer, pairs, inverse, amp, gap_rows,
    energy_out, energy_in,
    own_sem, index_sem, f_send, f_recv, w_send, w_recv, e_send, e_recv,
):
    aux_rows, columns = own.shape
    chunks = aux_rows // rows
    me = lax.axis_index("occ")
    right = lax.rem(me + 1, blocks)
    left = lax.rem(me + blocks - 1, blocks)

    own_copy = pltpu.make_async_copy(f_ref, own, own_sem)
    own_copy.start()
    index_copy = pltpu.make_async_copy(index_ref, gap_rows, index_sem)
    index_copy.start()

    barrier = pltpu.get_barrier_semaphore()

    def greet(step, carry):
        other = lax.rem(me + step, blocks)
        pl.semaphore_signal(barrier, inc=1, device_id={"occ": other}, device_id_type=MESH)
        return carry

    lax.fori_loop(1, blocks, greet, 0)
    pl.semaphore_wait(barrier, blocks - 1)

    def rows_of(step):
        return pl.ds(pl.multiple_of(step * rows, rows), rows)

    def f_copy(step):
        return pltpu.make_async_remote_copy(
            src_ref=f_ref.at[rows_of(step)], dst_ref=visiting.at[rows_of(step)],
            send_sem=f_send.at[step], recv_sem=f_recv.at[step],
            device_id={"occ": right}, device_id_type=MESH,
        )

    def w_copy(step):
        return pltpu.make_async_remote_copy(
            src_ref=outgoing.at[rows_of(step)], dst_ref=incoming.at[rows_of(step)],
            send_sem=w_send.at[step], recv_sem=w_recv.at[step],
            device_id={"occ": left}, device_id_type=MESH,
        )

    def e_copy(source, target):
        return pltpu.make_async_remote_copy(
            src_ref=energy_out.at[pl.ds(0, 1)], dst_ref=energy_in.at[source, pl.ds(0, 1)],
            send_sem=e_send.at[target], recv_sem=e_recv.at[source],
            device_id={"occ": target}, device_id_type=MESH,
        )

    @pl.loop(0, chunks)
    def _(step):
        f_copy(step).start()

    index_copy.wait()
    own_index = gap_rows[pl.ds(me, 1), :]
    partner_index = gap_rows[pl.ds(left, 1), :]
    zeros = jnp.zeros((1, columns), jnp.float32)

    def look_up(entry, gaps):
        value = table_ref[entry]
        return (
            jnp.where(own_index == entry, value, gaps[0]),
            jnp.where(partner_index == entry, value, gaps[1]),
        )

    own_gap, partner_gap = lax.fori_loop(0, table_ref.shape[0], look_up, (zeros, zeros))
    level = level_ref[me]
    shift = jnp.float32(0.0)
    for entry in range(shift_ref.shape[0]):
        shift = jnp.where(level == entry, shift_ref[entry], shift)
    own_column = jnp.transpose(jnp.broadcast_to(own_gap, (128, columns)))
    for start in range(0, columns, 128):
        part = pl.ds(start, 128)
        inverse[:, part] = 1.0 / (own_column + partner_gap[:, start : start + 128] + shift)

    pairs[...] = jnp.zeros_like(pairs)
    own_copy.wait()

    @pl.loop(0, chunks)
    def _(step):
        f_copy(step).wait_recv()
        pairs[...] += lax.dot_general(
            own[rows_of(step), :], visiting[rows_of(step), :], (((0,), (0,)), ((), ())),
            preferred_element_type=jnp.float32,
        )

    amp[...] = (pairs[...] * inverse[...]).astype(jnp.bfloat16)

    def send_w(step):
        outgoing[rows_of(step), :] = jnp.dot(
            own[rows_of(step), :], amp[...], preferred_element_type=jnp.float32
        ).astype(jnp.bfloat16)
        w_copy(step).start()

    send_w(0)
    pair = pairs[...]
    total = jnp.sum(pair * pair * inverse[...])
    energy_out[...] = jnp.full(energy_out.shape, total, jnp.float32)
    energy_in[me] = jnp.full(energy_out.shape, total, jnp.float32)

    @pl.loop(1, blocks)
    def _(step):
        e_copy(me, lax.rem(me + step, blocks)).start()

    @pl.loop(1, chunks)
    def _(step):
        send_w(step)

    @pl.loop(0, chunks)
    def _(step):
        nearer[rows_of(step), :] = lax.dot_general(
            visiting[rows_of(step), :], amp[...], (((1,), (1,)), ((), ())),
            preferred_element_type=jnp.float32,
        )

    @pl.loop(1, blocks)
    def _(step):
        e_copy(lax.rem(me + step, blocks), lax.rem(me + step, blocks)).wait_recv()

    energy_sum = energy_in[0]
    for block in range(1, blocks):
        energy_sum = energy_sum + energy_in[block]
    energy_ref[0] = energy_sum[0, 0] * scale

    @pl.loop(0, chunks)
    def _(step):
        f_copy(step).wait_send()

    @pl.loop(1, blocks)
    def _(step):
        e_copy(me, lax.rem(me + step, blocks)).wait_send()

    @pl.loop(0, chunks)
    def _(step):
        w_copy(step).wait_recv()
        out_ref[rows_of(step), :] = (
            nearer[rows_of(step), :] + incoming[rows_of(step), :].astype(jnp.float32)
        ).astype(jnp.bfloat16)

    @pl.loop(0, chunks)
    def _(step):
        w_copy(step).wait_send()


def on_device(factors, gap_index, gap_table, pair_level, pair_shift):
    aux_rows, occ_count, virtuals = factors.shape
    columns = occ_count * virtuals
    blocks = lax.axis_size("occ")
    rows = chunk_rows_of(aux_rows)
    chunks = aux_rows // rows
    scale = -1.3 / (blocks * STEPS * columns * columns)
    gradient, pair_energy = pl.pallas_call(
        functools.partial(kernel, blocks, rows, scale),
        out_shape=(
            OUT_SPACE((aux_rows, columns), jnp.bfloat16),
            jax.ShapeDtypeStruct((1,), jnp.float32),
        ),
        in_specs=[
            pl.BlockSpec(memory_space=pl.ANY),
            pl.BlockSpec(memory_space=pl.ANY),
            pl.BlockSpec(memory_space=pltpu.SMEM),
            pl.BlockSpec(memory_space=pltpu.SMEM),
            pl.BlockSpec(memory_space=pltpu.SMEM),
        ],
        out_specs=(
            pl.BlockSpec(memory_space=pltpu.VMEM),
            pl.BlockSpec(memory_space=pltpu.SMEM),
        ),
        scratch_shapes=[
            pltpu.VMEM((aux_rows, columns), jnp.bfloat16),
            pltpu.VMEM((aux_rows, columns), jnp.bfloat16),
            pltpu.VMEM((aux_rows, columns), jnp.bfloat16),
            pltpu.VMEM((aux_rows, columns), jnp.bfloat16),
            pltpu.VMEM((aux_rows, columns), jnp.float32),
            pltpu.VMEM((columns, columns), jnp.float32),
            pltpu.VMEM((columns, columns), jnp.float32),
            pltpu.VMEM((columns, columns), jnp.bfloat16),
            pltpu.VMEM((blocks, columns), jnp.int32),
            pltpu.VMEM((8, 128), jnp.float32),
            pltpu.VMEM((blocks, 8, 128), jnp.float32),
            pltpu.SemaphoreType.DMA,
            pltpu.SemaphoreType.DMA,
            pltpu.SemaphoreType.DMA((chunks,)),
            pltpu.SemaphoreType.DMA((chunks,)),
            pltpu.SemaphoreType.DMA((chunks,)),
            pltpu.SemaphoreType.DMA((chunks,)),
            pltpu.SemaphoreType.DMA((blocks,)),
            pltpu.SemaphoreType.DMA((blocks,)),
        ],
        compiler_params=pltpu.CompilerParams(
            collective_id=0, has_side_effects=True, vmem_limit_bytes=56 * 1024 * 1024
        ),
    )(
        factors.reshape(aux_rows, columns),
        gap_index.reshape(blocks, columns),
        gap_table,
        pair_level.reshape(-1),
        pair_shift,
    )
    return gradient.reshape(aux_rows, occ_count, virtuals), pair_energy


OUT_SPACE = pltpu.VMEM


def solution(mesh):
    in_specs = (P("cell", "occ", None), P("cell", None), P("cell"), P("cell", None), P())
    out_specs = (P("cell", "occ", None), P("cell"))
    return jax.shard_map(
        on_device, mesh=mesh, in_specs=in_specs, out_specs=out_specs, check_vma=False
    )
```

time: 209 us -> 154 us (0.74)
  the two profiles are of different devices: /device:TPU:0 before, /device:TPU:1 now
where the time goes in v1:
time: 154 us
  Pallas kernels  149 us (97%)
  local copies, waits for them, and re-layouts  2.71 us (2%)
  between operations  2.33 us (2%)
    pallas_call x1, Pallas kernels, on_device(): pl.pallas_call(functools.partial(kernel, blocks, rows, scale), out_shape=...  149 us

profile of v1, /device:TPU:1, one launch (start us, length us, event | category | flops | bytes accessed | tf_op | source)
XLA Modules:
  0.0 154.2 jit_solution(385404696605382836)
XLA Ops:
  0.6 149.2 %shard_map.68 = (bf16[6144,512]{1,0:T(8,128)(2,1)S(1)}, f32[1]{0:T(128)}) custom-call(bf16[6144,512]{1,0:T(8,128)(2,1)} %bitcast.4, s32[16,512]{1,0:T(8,128)} %index_ref.1, f32[64]{0:T(128)} %table_ref.1, s32[16]{0:T(128)} %bitcast.5, f32[8]{0:T(128)} %shift_ref.1), custom_call_target="tpu_custom_call" | custom-call | tf_op jit(solution)/shard_map/pallas_call | solution.py:177
  149.9 2.7 %copy.9 = bf16[6144,1,512]{2,0,1:T(8,128)(2,1)} copy(bf16[6144,1,512]{2,0,1:T(8,128)(2,1)S(1)} %bitcast.3) | data formatting | bytes 12582912

commit v2 on v1

--- a/solution.py
+++ b/solution.py
@@ -9,7 +9,8 @@
 
 STEPS = 1
 MESH = pl.DeviceIdType.MESH
-CHUNK_ROWS = 128
+CHUNK_ROWS = 256
+EARLY = 4
 
 
 def chunk_rows_of(aux_rows):
@@ -19,8 +20,12 @@
     return rows
 
 
+def part_columns_of(columns):
+    return columns // 2 if columns % 256 == 0 else columns
+
+
 def kernel(
-    blocks, rows, scale,
+    blocks, rows, width, scale,
     f_ref, index_ref, table_ref, level_ref, shift_ref,
     out_ref, energy_ref,
     own, visiting, outgoing, incoming, nearer, pairs, inverse, amp, gap_rows,
@@ -48,20 +53,27 @@
     lax.fori_loop(1, blocks, greet, 0)
     pl.semaphore_wait(barrier, blocks - 1)
 
+    parts = columns // width
+
     def rows_of(step):
         return pl.ds(pl.multiple_of(step * rows, rows), rows)
 
-    def f_copy(step):
+    def columns_of(part):
+        return pl.ds(part * width, width)
+
+    def f_copy(part, step):
         return pltpu.make_async_remote_copy(
-            src_ref=f_ref.at[rows_of(step)], dst_ref=visiting.at[rows_of(step)],
-            send_sem=f_send.at[step], recv_sem=f_recv.at[step],
+            src_ref=f_ref.at[rows_of(step), columns_of(part)],
+            dst_ref=visiting.at[rows_of(step), columns_of(part)],
+            send_sem=f_send.at[part, step], recv_sem=f_recv.at[part, step],
             device_id={"occ": right}, device_id_type=MESH,
         )
 
-    def w_copy(step):
+    def w_copy(part, step):
         return pltpu.make_async_remote_copy(
-            src_ref=outgoing.at[rows_of(step)], dst_ref=incoming.at[rows_of(step)],
-            send_sem=w_send.at[step], recv_sem=w_recv.at[step],
+            src_ref=outgoing.at[rows_of(step), columns_of(part)],
+            dst_ref=incoming.at[rows_of(step), columns_of(part)],
+            send_sem=w_send.at[part, step], recv_sem=w_recv.at[part, step],
             device_id={"occ": left}, device_id_type=MESH,
         )
 
@@ -72,9 +84,10 @@
             device_id={"occ": target}, device_id_type=MESH,
         )
 
-    @pl.loop(0, chunks)
-    def _(step):
-        f_copy(step).start()
+    for part in range(parts):
+        @pl.loop(0, chunks)
+        def _(step):
+            f_copy(part, step).start()
 
     index_copy.wait()
     own_index = gap_rows[pl.ds(me, 1), :]
@@ -101,21 +114,55 @@
     pairs[...] = jnp.zeros_like(pairs)
     own_copy.wait()
 
-    @pl.loop(0, chunks)
-    def _(step):
-        f_copy(step).wait_recv()
-        pairs[...] += lax.dot_general(
-            own[rows_of(step), :], visiting[rows_of(step), :], (((0,), (0,)), ((), ())),
+    def add_pairs(part, step):
+        f_copy(part, step).wait_recv()
+        pairs[:, columns_of(part)] += lax.dot_general(
+            own[rows_of(step), :], visiting[rows_of(step), columns_of(part)], (((0,), (0,)), ((), ())),
             preferred_element_type=jnp.float32,
         )
 
-    amp[...] = (pairs[...] * inverse[...]).astype(jnp.bfloat16)
+    def form_amp(part):
+        amp[:, columns_of(part)] = (
+            pairs[:, columns_of(part)] * inverse[:, columns_of(part)]
+        ).astype(jnp.bfloat16)
+
+    def form_w(part, step):
+        outgoing[rows_of(step), columns_of(part)] = jnp.dot(
+            own[rows_of(step), :], amp[:, columns_of(part)], preferred_element_type=jnp.float32
+        ).astype(jnp.bfloat16)
+
+    for part in range(parts - 1):
+        @pl.loop(0, chunks)
+        def _(step):
+            add_pairs(part, step)
+
+        form_amp(part)
+
+        @pl.loop(0, chunks)
+        def _(step):
+            form_w(part, step)
+
+    last = parts - 1
+    early = max(chunks - EARLY, 0)
+
+    @pl.loop(0, early)
+    def _(step):
+        add_pairs(last, step)
+
+    for part in range(last):
+        @pl.loop(0, chunks)
+        def _(step):
+            w_copy(part, step).start()
+
+    @pl.loop(early, chunks)
+    def _(step):
+        add_pairs(last, step)
+
+    form_amp(last)
 
     def send_w(step):
-        outgoing[rows_of(step), :] = jnp.dot(
-            own[rows_of(step), :], amp[...], preferred_element_type=jnp.float32
-        ).astype(jnp.bfloat16)
-        w_copy(step).start()
+        form_w(last, step)
+        w_copy(last, step).start()
 
     send_w(0)
     pair = pairs[...]
@@ -147,24 +194,28 @@
         energy_sum = energy_sum + energy_in[block]
     energy_ref[0] = energy_sum[0, 0] * scale
 
-    @pl.loop(0, chunks)
-    def _(step):
-        f_copy(step).wait_send()
+    for part in range(parts):
+        @pl.loop(0, chunks)
+        def _(step):
+            f_copy(part, step).wait_send()
 
     @pl.loop(1, blocks)
     def _(step):
         e_copy(me, lax.rem(me + step, blocks)).wait_send()
 
-    @pl.loop(0, chunks)
-    def _(step):
-        w_copy(step).wait_recv()
-        out_ref[rows_of(step), :] = (
-            nearer[rows_of(step), :] + incoming[rows_of(step), :].astype(jnp.float32)
-        ).astype(jnp.bfloat16)
-
-    @pl.loop(0, chunks)
-    def _(step):
-        w_copy(step).wait_send()
+    for part in range(parts):
+        @pl.loop(0, chunks)
+        def _(step):
+            w_copy(part, step).wait_recv()
+            out_ref[rows_of(step), columns_of(part)] = (
+                nearer[rows_of(step), columns_of(part)]
+                + incoming[rows_of(step), columns_of(part)].astype(jnp.float32)
+            ).astype(jnp.bfloat16)
+
+    for part in range(parts):
+        @pl.loop(0, chunks)
+        def _(step):
+            w_copy(part, step).wait_send()
 
 
 def on_device(factors, gap_index, gap_table, pair_level, pair_shift):
@@ -173,9 +224,11 @@
     blocks = lax.axis_size("occ")
     rows = chunk_rows_of(aux_rows)
     chunks = aux_rows // rows
+    width = part_columns_of(columns)
+    parts = columns // width
     scale = -1.3 / (blocks * STEPS * columns * columns)
     gradient, pair_energy = pl.pallas_call(
-        functools.partial(kernel, blocks, rows, scale),
+        functools.partial(kernel, blocks, rows, width, scale),
         out_shape=(
             OUT_SPACE((aux_rows, columns), jnp.bfloat16),
             jax.ShapeDtypeStruct((1,), jnp.float32),
@@ -205,10 +258,10 @@
             pltpu.VMEM((blocks, 8, 128), jnp.float32),
             pltpu.SemaphoreType.DMA,
             pltpu.SemaphoreType.DMA,
-            pltpu.SemaphoreType.DMA((chunks,)),
-            pltpu.SemaphoreType.DMA((chunks,)),
-            pltpu.SemaphoreType.DMA((chunks,)),
-            pltpu.SemaphoreType.DMA((chunks,)),
+            pltpu.SemaphoreType.DMA((parts, chunks)),
+            pltpu.SemaphoreType.DMA((parts, chunks)),
+            pltpu.SemaphoreType.DMA((parts, chunks)),
+            pltpu.SemaphoreType.DMA((parts, chunks)),
             pltpu.SemaphoreType.DMA((blocks,)),
             pltpu.SemaphoreType.DMA((blocks,)),
         ],

time: 154 us -> 188 us (1.22)
  Pallas kernels: 149 us -> 183 us
    pallas_call x1, Pallas kernels: 149 us -> 183 us  [on_device(): pl.pallas_call(functools.partial(kernel, blocks, rows, width, scale), out...]
where the time goes in v2:
time: 188 us
  Pallas kernels  183 us (97%)
  local copies, waits for them, and re-layouts  2.71 us (1%)
  between operations  2.33 us (1%)
    pallas_call x1, Pallas kernels, on_device(): pl.pallas_call(functools.partial(kernel, blocks, rows, width, scale), out...  183 us

profile of v2, /device:TPU:1, one launch (start us, length us, event | category | flops | bytes accessed | tf_op | source)
XLA Modules:
  0.0 188.0 jit_solution(12528532471291203868)
XLA Ops:
  0.6 182.9 %shard_map.68 = (bf16[6144,512]{1,0:T(8,128)(2,1)S(1)}, f32[1]{0:T(128)}) custom-call(bf16[6144,512]{1,0:T(8,128)(2,1)} %bitcast.4, s32[16,512]{1,0:T(8,128)} %index_ref.1, f32[64]{0:T(128)} %table_ref.1, s32[16]{0:T(128)} %bitcast.5, f32[8]{0:T(128)} %shift_ref.1), custom_call_target="tpu_custom_call" | custom-call | tf_op jit(solution)/shard_map/pallas_call | solution.py:230
  183.6 2.7 %copy.9 = bf16[6144,1,512]{2,0,1:T(8,128)(2,1)} copy(bf16[6144,1,512]{2,0,1:T(8,128)(2,1)S(1)} %bitcast.3) | data formatting | bytes 12582912

commit v3 on v2

--- a/solution.py
+++ b/solution.py
@@ -9,8 +9,9 @@
 
 STEPS = 1
 MESH = pl.DeviceIdType.MESH
-CHUNK_ROWS = 256
-EARLY = 4
+CHUNK_ROWS = 512
+EARLY = 2
+IN_FLIGHT = 0
 
 
 def chunk_rows_of(aux_rows):
@@ -22,6 +23,13 @@
 
 def part_columns_of(columns):
     return columns // 2 if columns % 256 == 0 else columns
+
+
+def stages_of(blocks):
+    stages = 0
+    while 2**stages < blocks // 2:
+        stages += 1
+    return stages
 
 
 def kernel(
@@ -30,7 +38,7 @@
     out_ref, energy_ref,
     own, visiting, outgoing, incoming, nearer, pairs, inverse, amp, gap_rows,
     energy_out, energy_in,
-    own_sem, index_sem, f_send, f_recv, w_send, w_recv, e_send, e_recv,
+    own_sem, index_sem, f_send, f_recv, w_send, w_recv, e_send, e_recv, f_left, started,
 ):
     aux_rows, columns = own.shape
     chunks = aux_rows // rows
@@ -45,13 +53,9 @@
 
     barrier = pltpu.get_barrier_semaphore()
 
-    def greet(step, carry):
-        other = lax.rem(me + step, blocks)
+    for other in (left, right):
         pl.semaphore_signal(barrier, inc=1, device_id={"occ": other}, device_id_type=MESH)
-        return carry
-
-    lax.fori_loop(1, blocks, greet, 0)
-    pl.semaphore_wait(barrier, blocks - 1)
+    pl.semaphore_wait(barrier, 2)
 
     parts = columns // width
 
@@ -114,6 +118,12 @@
     pairs[...] = jnp.zeros_like(pairs)
     own_copy.wait()
 
+    for stage in range(stages_of(blocks)):
+        reach = 2**stage
+        for other in (lax.rem(me + reach, blocks), lax.rem(me + blocks - reach, blocks)):
+            pl.semaphore_signal(started.at[stage], inc=1, device_id={"occ": other}, device_id_type=MESH)
+        pl.semaphore_wait(started.at[stage], 2)
+
     def add_pairs(part, step):
         f_copy(part, step).wait_recv()
         pairs[:, columns_of(part)] += lax.dot_general(
@@ -144,10 +154,19 @@
 
     last = parts - 1
     early = max(chunks - EARLY, 0)
+    in_flight = min(IN_FLIGHT, chunks)
 
     @pl.loop(0, early)
     def _(step):
         add_pairs(last, step)
+
+    for part in range(parts):
+        @pl.loop(0, chunks if part < last else chunks - in_flight)
+        def _(step):
+            f_copy(part, step).wait_send()
+
+    pl.semaphore_signal(f_left, inc=1, device_id={"occ": left}, device_id_type=MESH)
+    pl.semaphore_wait(f_left, 1)
 
     for part in range(last):
         @pl.loop(0, chunks)
@@ -194,10 +213,9 @@
         energy_sum = energy_sum + energy_in[block]
     energy_ref[0] = energy_sum[0, 0] * scale
 
-    for part in range(parts):
-        @pl.loop(0, chunks)
-        def _(step):
-            f_copy(part, step).wait_send()
+    @pl.loop(chunks - in_flight, chunks)
+    def _(step):
+        f_copy(last, step).wait_send()
 
     @pl.loop(1, blocks)
     def _(step):
@@ -264,6 +282,8 @@
             pltpu.SemaphoreType.DMA((parts, chunks)),
             pltpu.SemaphoreType.DMA((blocks,)),
             pltpu.SemaphoreType.DMA((blocks,)),
+            pltpu.SemaphoreType.REGULAR,
+            pltpu.SemaphoreType.REGULAR((max(stages_of(blocks), 1),)),
         ],
         compiler_params=pltpu.CompilerParams(
             collective_id=0, has_side_effects=True, vmem_limit_bytes=56 * 1024 * 1024

time: 188 us -> 150 us (0.80)
  Pallas kernels: 183 us -> 144 us
    pallas_call x1, Pallas kernels: 183 us -> 144 us  [on_device(): pl.pallas_call(functools.partial(kernel, blocks, rows, width, scale), out...]
where the time goes in v3:
time: 150 us
  Pallas kernels  144 us (96%)
  local copies, waits for them, and re-layouts  2.71 us (2%)
  between operations  2.33 us (2%)
    pallas_call x1, Pallas kernels, on_device(): pl.pallas_call(functools.partial(kernel, blocks, rows, width, scale), out...  144 us

profile of v3, /device:TPU:1, one launch (start us, length us, event | category | flops | bytes accessed | tf_op | source)
XLA Modules:
  0.0 149.5 jit_solution(14417544909837796246)
XLA Ops:
  0.6 144.5 %shard_map.68 = (bf16[6144,512]{1,0:T(8,128)(2,1)S(1)}, f32[1]{0:T(128)}) custom-call(bf16[6144,512]{1,0:T(8,128)(2,1)} %bitcast.4, s32[16,512]{1,0:T(8,128)} %index_ref.1, f32[64]{0:T(128)} %table_ref.1, s32[16]{0:T(128)} %bitcast.5, f32[8]{0:T(128)} %shift_ref.1), custom_call_target="tpu_custom_call" | custom-call | tf_op jit(solution)/shard_map/pallas_call | solution.py:248
  145.1 2.7 %copy.9 = bf16[6144,1,512]{2,0,1:T(8,128)(2,1)} copy(bf16[6144,1,512]{2,0,1:T(8,128)(2,1)S(1)} %bitcast.3) | data formatting | bytes 12582912

commit v4 on v3

--- a/solution.py
+++ b/solution.py
@@ -9,7 +9,7 @@
 
 STEPS = 1
 MESH = pl.DeviceIdType.MESH
-CHUNK_ROWS = 512
+CHUNK_ROWS = 1024
 EARLY = 2
 IN_FLIGHT = 0
 

time: 150 us -> 149 us (level)
  no operation moved by 1% of the time
where the time goes in v4:
time: 149 us
  Pallas kernels  144 us (97%)
  local copies, waits for them, and re-layouts  2.71 us (2%)
  between operations  2.33 us (2%)
    pallas_call x1, Pallas kernels, on_device(): pl.pallas_call(functools.partial(kernel, blocks, rows, width, scale), out...  144 us

profile of v4, /device:TPU:1, one launch (start us, length us, event | category | flops | bytes accessed | tf_op | source)
XLA Modules:
  0.0 149.1 jit_solution(2393073393465190632)
XLA Ops:
  0.6 144.0 %shard_map.68 = (bf16[6144,512]{1,0:T(8,128)(2,1)S(1)}, f32[1]{0:T(128)}) custom-call(bf16[6144,512]{1,0:T(8,128)(2,1)} %bitcast.4, s32[16,512]{1,0:T(8,128)} %index_ref.1, f32[64]{0:T(128)} %table_ref.1, s32[16]{0:T(128)} %bitcast.5, f32[8]{0:T(128)} %shift_ref.1), custom_call_target="tpu_custom_call" | custom-call | tf_op jit(solution)/shard_map/pallas_call | solution.py:248
  144.7 2.7 %copy.9 = bf16[6144,1,512]{2,0,1:T(8,128)(2,1)} copy(bf16[6144,1,512]{2,0,1:T(8,128)(2,1)S(1)} %bitcast.3) | data formatting | bytes 12582912
